TPU v7x, 512 devices: a whole 4x4x16 slice. The times are simulated.
512 devices in a mesh: row: 32 (over z, core), col: 16 (over y, x).
Axes of the slice: x: 4, y: 4, z: 16, core: 2. Of those that a mesh axis runs over, the one named last changes fastest.
Arguments:
- features: bfloat16 [16, 4096, 256], P('col', 'row'), may hold values from -6 to 6
- tiles: bfloat16 [32, 16, 56, 128, 128], P('row', 'col'), may hold values from -0.5 to 0.5
- tile_rows: int32 [32, 16, 56], P('row', 'col'), may hold values from 0 to 15, as said below
- tile_cols: int32 [32, 16, 56], P('row', 'col'), may hold values from 0 to 31, as said below
- tile_count: int32 [32, 16], P('row', 'col'), may hold values from 4 to 56, as said below
- weight: bfloat16 [256, 256], replicated, may hold values from -0.375 to 0.375
- bias: float32 [256], replicated, may hold values from -3 to 3
- cotangent: bfloat16 [32, 2048, 256], P('row', 'col'), may hold values from -6 to 6
- label_mask: int32 [32, 2048], P('row', 'col'), may hold values 0 or 1
Outputs:
- hidden: bfloat16 [32, 2048, 256], P('row', 'col')
- grad_weight: float32 [256, 256], replicated
- grad_bias: float32 [256], replicated
- grad_features: bfloat16 [16, 4096, 256], P('col', 'row')
Inputs may be any that keep to these rules, and one draw needn't show every extreme that they name: `tile_rows`: tile row among the 16 tile rows of a block; the (row, column) positions of one block's slots are all distinct. `tile_cols`: tile column among the 32 tile columns of a block. The live slots of a block are its first tile_count slots; some block has all 56 slots live.
All inputs are finite; a program needn't handle non-finite values. No bound on the sum of `label_mask` on one device may be relied on, other than what follows from the above.
Results may differ from a plain program's by a relative error of at most 0.023.
Values may be sent and summed in bfloat16 or wider, within the bound.
A program may use at most 64 MiB of HBM per device.

v0:
```python
import math
import jax
import jax.numpy as jnp
from jax import lax
from jax.sharding import PartitionSpec as P


def tile_products(block_tiles, take_index, put_index, live_count, source, out_tiles, transpose):
    total_slots = block_tiles.shape[0]
    group = math.gcd(total_slots, 16)
    tile_size = block_tiles.shape[1]
    width = source.shape[-1]
    form = "sij,sif->sjf" if transpose else "sij,sjf->sif"

    def step(turn, accum):
        start = turn * group
        block = lax.dynamic_slice_in_dim(block_tiles, start, group, 0)
        take = lax.dynamic_slice_in_dim(take_index, start, group, 0)
        put = lax.dynamic_slice_in_dim(put_index, start, group, 0)
        live = start + jnp.arange(group, dtype=jnp.int32) < live_count
        picked = jnp.take(source, take, axis=0)
        product = jnp.einsum(form, block, picked, preferred_element_type=jnp.float32)
        product = jnp.where(live[:, None, None], product, 0.0)
        return accum.at[put].add(product)

    turns = (live_count + group - 1) // group
    start_value = jnp.zeros((out_tiles, tile_size, width), jnp.float32)
    return lax.fori_loop(0, turns, step, start_value)


def times_weight_t(values, weight):
    return lax.dot_general(
        values, weight, (((1,), (1,)), ((), ())), preferred_element_type=jnp.float32
    ).astype(jnp.bfloat16)


def on_device(
    features, tiles, tile_rows, tile_cols, tile_count, weight, bias, cotangent, label_mask
):
    tile_size = tiles.shape[-1]
    rows_dev = features.shape[1]
    width = features.shape[2]
    n_row = lax.axis_size("row")
    n_col = lax.axis_size("col")
    own_tiles = tiles[0, 0]
    rows_index = tile_rows[0, 0]
    cols_index = tile_cols[0, 0]
    live_count = tile_count[0, 0]
    gathered = lax.all_gather(features, "row", axis=1, tiled=True)
    source = gathered.reshape(n_row * rows_dev // tile_size, tile_size, width)
    partial_value = tile_products(
        own_tiles, cols_index, rows_index, live_count, source, n_col * rows_dev // tile_size, False
    )
    partial_value = partial_value.reshape(n_col * rows_dev, width)
    summed = lax.psum_scatter(
        partial_value.astype(jnp.bfloat16), "col", scatter_dimension=0, tiled=True
    )
    pre_act = jnp.dot(summed, weight, preferred_element_type=jnp.float32) + bias
    sigma = jax.nn.sigmoid(pre_act)
    hidden = (pre_act * sigma).astype(jnp.bfloat16)
    kept = label_mask[0].astype(jnp.float32)[:, None]
    slope = sigma * (1.0 + pre_act * (1.0 - sigma))
    grad_pre = (cotangent[0].astype(jnp.float32) * kept * slope).astype(jnp.bfloat16)
    local_weight = lax.dot_general(
        summed, grad_pre, (((0,), (0,)), ((), ())), preferred_element_type=jnp.float32
    )
    local_bias = jnp.sum(grad_pre.astype(jnp.float32), axis=0)
    grad_weight, grad_bias = lax.psum((local_weight, local_bias), ("row", "col"))
    scale = 1.0 / math.sqrt(n_row * n_col * rows_dev)
    grad_agg = times_weight_t(grad_pre, weight)
    grad_rows = lax.all_gather(grad_agg[None], "col", axis=1, tiled=True)[0]
    back_source = grad_rows.reshape(n_col * rows_dev // tile_size, tile_size, width)
    back = tile_products(
        own_tiles,
        rows_index,
        cols_index,
        live_count,
        back_source,
        n_row * rows_dev // tile_size,
        True,
    )
    back = back.reshape(n_row * rows_dev, width)
    back = lax.optimization_barrier(back.astype(jnp.bfloat16)).astype(jnp.float32)
    grad_sum = lax.psum_scatter(back.astype(jnp.bfloat16), "row", scatter_dimension=0, tiled=True)
    return (hidden[None], grad_weight * scale, grad_bias * scale, grad_sum[None])


def solution(mesh):
    return jax.shard_map(
        on_device,
        mesh=mesh,
        in_specs=(
            P("col", "row", None),
            P("row", "col", None, None, None),
            P("row", "col", None),
            P("row", "col", None),
            P("row", "col"),
            P(),
            P(),
            P("row", "col", None),
            P("row", "col"),
        ),
        out_specs=(P("row", "col", None), P(), P(), P("col", "row", None)),
        check_vma=False,
    )
```

profile of v0, /device:TPU:16, one launch (start us, length us, event | category | flops | bytes accessed | tf_op | source)
XLA Modules:
  0.0 869.9 jit_solution(1376284081427758743)
XLA Ops:
  7.2 0.0 copy-start
  7.2 0.0 copy-start.4
  7.2 0.0 copy-start.5
  7.2 0.0 copy-start.2
  7.2 0.0 all-gather.4.cloned.1.call-start
  7.3 0.7 all-gather.4.cloned.1.call-update
  7.9 0.0 reduce-scatter.3.cloned.1.call-start
  8.7 77.2 %all-gather.4.cloned.1.call-done = bf16[1,4096,256]{2,1,0:T(8,128)(2,1)} async-done(((bf16[1,128,256]{2,1,0:T(8,128)(2,1)}), bf16[1,4096,256]{2,1,0:T(8,128)(2,1)}) %all-gather.4.cloned.1.call-update) | async-done | bytes 2097168 | tf_op jit(solution)/shard_map/all_gather | solution.py:49
  85.9 1.5 broadcast_in_dim.69
  87.4 0.0 copy-done.4
  87.4 0.0 copy-done.5
  87.4 0.0 copy-done.2
  87.4 6.7 while.20
  87.5 0.7 compare_and_fusion.4
  88.2 2.2 gather_fusion
  90.4 0.4 convolution_select_fusion.4
  90.7 0.1 compare_select_fusion.8
  90.8 3.3 scatter_fusion
  94.1 0.0 copy-start.8
  94.1 0.0 copy-start.6
  94.1 0.0 copy-start.7
  94.1 2.7 convert_element_type.42
  96.8 0.0 reduce-scatter.3.cloned.1.call-update
  96.9 0.0 all-gather.6.cloned.1.call-start
  96.9 0.0 copy-done.8
  96.9 122.7 %reduce-scatter.3.cloned.1.call-done = bf16[128,256]{1,0:T(8,128)(2,1)} async-done(((bf16[2048,256]{1,0:T(8,128)(2,1)}), bf16[128,256]{1,0:T(8,128)(2,1)}) %reduce-scatter.3.cloned.1.call-update) | async-done | bytes 65552 | tf_op jit(solution)/shard_map/reduce_scatter | solution.py:55
  219.6 0.0 copy-done
  219.7 0.0 copy-done.6
  219.7 0.0 copy-done.7
  219.7 1.7 convert_reduce_fusion
  221.3 0.0 copy-start.3
  221.3 0.8 convolution_convert_fusion
  222.2 0.0 all-gather.6.cloned.1.call-update
  222.2 0.0 all-reduce.2.cloned.1.call-start
  222.2 2.9 copy.13
  225.2 0.0 copy-done.3
  225.2 0.9 fusion.16
  226.1 0.0 all-reduce.2.cloned.1.call-update
  226.1 0.0 reduce-scatter.5.cloned.1.call-start
  226.2 54.1 %all-gather.6.cloned.1.call-done = bf16[2048,256]{1,0:T(8,128)(2,1)} async-done(((bf16[128,256]{1,0:T(8,128)(2,1)}), bf16[2048,256]{1,0:T(8,128)(2,1)}) %all-gather.6.cloned.1.call-update) | async-done | bytes 1048592 | tf_op jit(solution)/shard_map/all_gather | solution.py:71
  280.3 0.0 copy-start.1
  280.3 2.4 broadcast_in_dim.71
  282.7 0.0 copy-done.1
  282.7 6.0 while.21
  282.7 0.7 compare_and_fusion.5
  283.4 0.6 gather_fusion.1
  284.0 1.3 convolution_select_fusion.5
  285.3 0.1 compare_select_fusion.9
  285.4 3.3 scatter_fusion.1
  288.7 3.8 convert_element_type.52
  292.5 0.0 reduce-scatter.5.cloned.1.call-update
  292.5 136.9 %psum.15 = f32[256]{0:T(256)S(1)} all-reduce(f32[256]{0:T(256)S(1)} %get-tuple-element.136), channel_id=1, replica_groups=mesh['row'=32,'col'=16] {'row','col'}, use_global_device_ids=true, to_apply=%region_6.7 | all-reduce | flops 256 | bytes 2048 | tf_op jit(solution)/shard_map/psum | solution.py:68
  429.4 0.6 broadcast_multiply_fusion.1
  430.0 322.5 %all-reduce.2.cloned.1.call-done = f32[256,256]{1,0:T(8,128)} async-done(((f32[256,256]{1,0:T(8,128)}), f32[256,256]{1,0:T(8,128)}) %all-reduce.2.cloned.1.call-update) | async-done | bytes 262160 | tf_op jit(solution)/shard_map/psum | solution.py:68
  752.5 1.7 broadcast_multiply_fusion
  754.2 109.2 %reduce-scatter.5.cloned.1.call-done = bf16[128,256]{1,0:T(8,128)(2,1)} async-done(((bf16[4096,256]{1,0:T(8,128)(2,1)}), bf16[128,256]{1,0:T(8,128)(2,1)}) %reduce-scatter.5.cloned.1.call-update) | async-done | bytes 65552 | tf_op jit(solution)/shard_map/reduce_scatter | solution.py:84
  (3 shorter events, 0.0 us)
Async XLA Ops:
  7.2 212.5 %copy-start = (bf16[256,256]{1,0:T(8,128)(2,1)S(1)}, bf16[256,256]{1,0:T(8,128)(2,1)}, u32[]{:S(2)}) copy-start(bf16[256,256]{1,0:T(8,128)(2,1)} %param.18) | copy-start | bytes 393220
  7.2 80.3 %copy-start.4 = (s32[1,1,56]{2,1,0:T(1,128)S(1)}, s32[1,1,56]{2,1,0:T(1,128)}, u32[]{:S(2)}) copy-start(s32[1,1,56]{2,1,0:T(1,128)} %param.15) | copy-start | bytes 676
  7.2 80.2 %copy-start.5 = (s32[1,1,56]{2,1,0:T(1,128)S(1)}, s32[1,1,56]{2,1,0:T(1,128)}, u32[]{:S(2)}) copy-start(s32[1,1,56]{2,1,0:T(1,128)} %param.16) | copy-start | bytes 676
  7.2 80.2 %copy-start.2 = (bf16[1,1,56,128,128]{4,3,2,1,0:T(8,128)(2,1)S(1)}, bf16[1,1,56,128,128]{4,3,2,1,0:T(8,128)(2,1)}, u32[]{:S(2)}) copy-start(bf16[1,1,56,128,128]{4,3,2,1,0:T(8,128)(2,1)} %param.14) | copy-start | bytes 5505028
  7.2 78.7 %all-gather.4.cloned.1.call-start = ((), (), s32[]{:S(2)}) async-start(), calls=%async_computation.2 | async-start | bytes 2162688 | tf_op jit(solution)/shard_map/all_gather | solution.py:49
  7.9 211.7 %reduce-scatter.3.cloned.1.call-start = ((), (), s32[]{:S(2)}) async-start(), calls=%async_computation.3 | async-start | bytes 1114112 | tf_op jit(solution)/shard_map/reduce_scatter | solution.py:55
  94.1 2.8 copy-start.8
  94.1 125.5 %copy-start.6 = (bf16[1,128,256]{2,1,0:T(8,128)(2,1)S(1)}, bf16[1,128,256]{2,1,0:T(8,128)(2,1)}, u32[]{:S(2)}) copy-start(bf16[1,128,256]{2,1,0:T(8,128)(2,1)} %param.20) | copy-start | bytes 196612
  94.1 125.5 %copy-start.7 = (f32[256]{0:T(256)S(1)}, f32[256]{0:T(256)}, u32[]{:S(2)}) copy-start(f32[256]{0:T(256)} %param.19) | copy-start | bytes 3076
  96.9 183.4 %all-gather.6.cloned.1.call-start = ((), (), s32[]{:S(2)}) async-start(), calls=%async_computation.6 | async-start | bytes 1114112 | tf_op jit(solution)/shard_map/all_gather | solution.py:71
  221.3 3.8 copy-start.3
  222.2 530.3 %all-reduce.2.cloned.1.call-start = ((), (), s32[]{:S(2)}) async-start(), calls=%async_computation.4 | async-start | bytes 524288 | tf_op jit(solution)/shard_map/psum | solution.py:68
  226.1 637.3 %reduce-scatter.5.cloned.1.call-start = ((), (), s32[]{:S(2)}) async-start(), calls=%async_computation.5 | async-start | bytes 2162688 | tf_op jit(solution)/shard_map/reduce_scatter | solution.py:84
  280.3 2.4 copy-start.1
Sparse Core Ops, SparseCore 0:
  10.1 75.7 all-gather.3
  97.0 122.6 reduce-scatter.2
  223.2 56.9 all-gather.5
  286.1 466.3 all-reduce.1
  755.7 107.6 reduce-scatter.4
where the time goes:
time: 871 us; the launch traced here: 870 us
  waiting for transfers between devices  687 us (79%)
  blocking collectives  137 us (16%)
  other arithmetic  16.9 us (2%)
  between operations  14.5 us (2%)
  local copies, waits for them, and re-layouts  9.66 us (1%)
    psum x1, waiting for transfers between devices, on_device(): lax.psum((local_weight, local_bias), ('row', 'col'))  323 us
    psum x1, blocking collectives, on_device(): lax.psum((local_weight, local_bias), ('row', 'col'))  137 us
    reduce_scatter x1, waiting for transfers between devices, on_device(): lax.psum_scatter(partial_value.astype(jnp.bfloat16), 'col', scatter_dimen...  123 us
    reduce_scatter x1, waiting for transfers between devices, on_device(): lax.psum_scatter(back.astype(jnp.bfloat16), 'row', scatter_dimension=0, t...  109 us
    all_gather x1, waiting for transfers between devices, on_device(): gathered = lax.all_gather(features, 'row', axis=1, tiled=True)  77.2 us
    all_gather x1, waiting for transfers between devices, on_device(): grad_rows = lax.all_gather(grad_agg[None], 'col', axis=1, tiled=True)[0]  54.1 us
  transfers between devices with their start and end apart: 5, of which 5 were waited for; matrix products, arithmetic and copies ran while one was open for 2% of the time, Pallas kernels for 0%

commit v1 on v0

--- a/solution.py
+++ b/solution.py
@@ -37,6 +37,11 @@
 def on_device(
     features, tiles, tile_rows, tile_cols, tile_count, weight, bias, cotangent, label_mask
 ):
+
+    def plan_tracks(content):
+        new = lax.psum(lax.psum(content, "row"), "col")
+        return new
+
     tile_size = tiles.shape[-1]
     rows_dev = features.shape[1]
     width = features.shape[2]
@@ -65,7 +70,7 @@
         summed, grad_pre, (((0,), (0,)), ((), ())), preferred_element_type=jnp.float32
     )
     local_bias = jnp.sum(grad_pre.astype(jnp.float32), axis=0)
-    grad_weight, grad_bias = lax.psum((local_weight, local_bias), ("row", "col"))
+    grad_weight, grad_bias = plan_tracks((local_weight, local_bias))
     scale = 1.0 / math.sqrt(n_row * n_col * rows_dev)
     grad_agg = times_weight_t(grad_pre, weight)
     grad_rows = lax.all_gather(grad_agg[None], "col", axis=1, tiled=True)[0]

time: 871 us -> 736 us (0.85)
  the two profiles are of different devices: /device:TPU:16 before, /device:TPU:4 now
where the time goes in v1:
time: 736 us; the launch traced here: 734 us
  waiting for transfers between devices  555 us (75%)
  blocking collectives  93.6 us (13%)
  other arithmetic  41.7 us (6%)
  local copies, waits for them, and re-layouts  17.9 us (2%)
  between operations  14.8 us (2%)
  matrix products  11 us (1%)
    psum x2, waiting for transfers between devices, plan_tracks(): new = lax.psum(lax.psum(content, 'row'), 'col')  206 us
    reduce_scatter x1, waiting for transfers between devices, on_device(): lax.psum_scatter(back.astype(jnp.bfloat16), 'row', scatter_dimension=0, t...  107 us
    reduce_scatter x1, waiting for transfers between devices, on_device(): lax.psum_scatter(partial_value.astype(jnp.bfloat16), 'col', scatter_dimen...  103 us
    psum x2, blocking collectives, plan_tracks(): new = lax.psum(lax.psum(content, 'row'), 'col')  93.6 us
    all_gather x1, waiting for transfers between devices, on_device(): gathered = lax.all_gather(features, 'row', axis=1, tiled=True)  77.4 us
    all_gather x1, waiting for transfers between devices, on_device(): grad_rows = lax.all_gather(grad_agg[None], 'col', axis=1, tiled=True)[0]  60.7 us
    scatter-add x8, other arithmetic, step(): return accum.at[put].add(product)  26.4 us
  transfers between devices with their start and end apart: 6, of which 5 were waited for; matrix products, arithmetic and copies ran while one was open for 5% of the time, Pallas kernels for 0%

profile of v1, /device:TPU:4, one launch (start us, length us, event | category | flops | bytes accessed | tf_op | source)
XLA Modules:
  0.0 734.5 jit_solution(2885548586579943033)
XLA Ops:
  7.3 0.7 all-gather.4.cloned.1.call-update
  7.9 0.0 reduce-scatter.3.cloned.1.call-start
  8.7 77.4 %all-gather.4.cloned.1.call-done = bf16[1,4096,256]{2,1,0:T(8,128)(2,1)} async-done(((bf16[1,128,256]{2,1,0:T(8,128)(2,1)}), bf16[1,4096,256]{2,1,0:T(8,128)(2,1)}) %all-gather.4.cloned.1.call-update) | async-done | bytes 2097168 | tf_op jit(solution)/shard_map/all_gather | solution.py:54
  86.0 1.5 broadcast_in_dim.69
  87.6 26.7 %while.20 = (s32[]{:T(128)}, f32[16,128,256]{2,1,0:T(8,128)}, s32[]{:T(128)}, s32[56]{0:T(128)S(1)}, s32[]{:T(128)}, /*index=5*/bf16[56,128,128]{2,1,0:T(8,128)(...) while((s32[]{:T(128)}, f32[16,128,256]{2,1,0:T(8,128)}, ...), condition=%wide.region_2.3_spmd, body=%wide.region_0.2_spmd.sunk | while | flops 67896416 | bytes 6034855 | solution.py:28
  87.6 0.7 compare_and_fusion.4
  88.3 2.2 gather_fusion
  90.5 0.4 convolution_select_fusion.4
  90.9 0.1 compare_select_fusion.8
  91.0 3.2 scatter_fusion
  94.2 0.7 compare_and_fusion.4
  94.9 2.2 gather_fusion
  97.1 0.4 convolution_select_fusion.4
  97.5 0.1 compare_select_fusion.8
  97.5 3.3 scatter_fusion
  100.8 0.7 compare_and_fusion.4
  101.6 2.2 gather_fusion
  103.7 0.4 convolution_select_fusion.4
  104.1 0.1 compare_select_fusion.8
  104.2 3.3 scatter_fusion
  107.5 0.7 compare_and_fusion.4
  108.3 2.2 gather_fusion
  110.5 0.4 convolution_select_fusion.4
  110.8 0.1 compare_select_fusion.8
  110.9 3.3 scatter_fusion
  114.2 2.7 convert_element_type.42
  117.0 0.0 all-reduce.3.cloned.1.call-start
  117.1 102.7 %reduce-scatter.3.cloned.1.call-done = bf16[128,256]{1,0:T(8,128)(2,1)} async-done(((bf16[2048,256]{1,0:T(8,128)(2,1)}), bf16[128,256]{1,0:T(8,128)(2,1)}) %reduce-scatter.3.cloned.1.call-update) | async-done | bytes 65552 | tf_op jit(solution)/shard_map/reduce_scatter | solution.py:60
  219.8 1.7 convert_reduce_fusion
  221.5 1.8 fusion.16
  223.3 0.0 all-gather.6.cloned.1.call-start
  223.3 0.8 convolution_convert_fusion
  224.2 0.0 all-reduce.5.cloned.1.call-start
  224.2 2.9 copy.13
  227.2 206.4 %all-reduce.3.cloned.1.call-done = f32[256,256]{1,0:T(8,128)} async-done(((f32[256,256]{1,0:T(8,128)}), f32[256,256]{1,0:T(8,128)}) %all-reduce.3.cloned.1.call-update) | async-done | bytes 262160 | tf_op jit(solution)/shard_map/psum | solution.py:42
  433.6 60.7 %all-gather.6.cloned.1.call-done = bf16[2048,256]{1,0:T(8,128)(2,1)} async-done(((bf16[128,256]{1,0:T(8,128)(2,1)}), bf16[2048,256]{1,0:T(8,128)(2,1)}) %all-gather.6.cloned.1.call-update) | async-done | bytes 1048592 | tf_op jit(solution)/shard_map/all_gather | solution.py:76
  494.4 2.4 broadcast_in_dim.71
  496.8 24.2 %while.21 = (s32[]{:T(128)}, f32[32,128,256]{2,1,0:T(8,128)}, s32[]{:T(128)}, s32[56]{0:T(128)S(1)}, s32[]{:T(128)}, /*index=5*/bf16[56,128,128]{1,2,0:T(8,128)(...) while((s32[]{:T(128)}, f32[32,128,256]{2,1,0:T(8,128)}, ...), condition=%wide.region_11.12_spmd, body=%wide.region_9.11_spmd.sunk | while | flops 67896416 | bytes 6033847 | solution.py:28
  496.8 0.7 compare_and_fusion.5
  497.5 0.6 gather_fusion.1
  498.1 1.3 convolution_select_fusion.5
  499.4 0.1 compare_select_fusion.9
  499.5 3.3 scatter_fusion.1
  502.9 0.7 compare_and_fusion.5
  503.6 0.6 gather_fusion.1
  504.2 1.3 convolution_select_fusion.5
  505.5 0.1 compare_select_fusion.9
  505.6 3.3 scatter_fusion.1
  508.9 0.7 compare_and_fusion.5
  509.6 0.6 gather_fusion.1
  510.2 1.3 convolution_select_fusion.5
  511.5 0.1 compare_select_fusion.9
  511.6 3.4 scatter_fusion.1
  515.0 0.7 compare_and_fusion.5
  515.7 0.6 gather_fusion.1
  516.3 1.3 convolution_select_fusion.5
  517.6 0.1 compare_select_fusion.9
  517.7 3.3 scatter_fusion.1
  521.0 3.8 convert_element_type.52
  524.8 50.7 %psum.30 = f32[256]{0:T(256)S(1)} all-reduce(f32[256]{0:T(256)S(1)} %get-tuple-element.136), channel_id=1, replica_groups=mesh['row'=32,'col'=16] {'row'}, use_global_device_ids=true, to_apply=%region_7.8 | all-reduce | flops 256 | bytes 2048 | tf_op jit(solution)/shard_map/psum | solution.py:42
  575.5 42.9 %psum.31 = f32[256]{0:T(256)S(1)} all-reduce(f32[256]{0:T(256)S(1)} %psum.30), channel_id=1, replica_groups=mesh['row'=32,'col'=16] {'col'}, use_global_device_ids=true, to_apply=%region_8.9 | all-reduce | flops 256 | bytes 2048 | tf_op jit(solution)/shard_map/psum | solution.py:42
  618.4 0.6 broadcast_multiply_fusion.1
  619.0 1.7 broadcast_multiply_fusion
  620.7 106.9 %reduce-scatter.5.cloned.1.call-done = bf16[128,256]{1,0:T(8,128)(2,1)} async-done(((bf16[4096,256]{1,0:T(8,128)(2,1)}), bf16[128,256]{1,0:T(8,128)(2,1)}) %reduce-scatter.5.cloned.1.call-update) | async-done | bytes 65552 | tf_op jit(solution)/shard_map/reduce_scatter | solution.py:89
  (33 shorter events, 0.2 us)
Async XLA Ops:
  7.2 212.6 %copy-start = (bf16[256,256]{1,0:T(8,128)(2,1)S(1)}, bf16[256,256]{1,0:T(8,128)(2,1)}, u32[]{:S(2)}) copy-start(bf16[256,256]{1,0:T(8,128)(2,1)} %param.18) | copy-start | bytes 393220
  7.2 80.4 %copy-start.3 = (s32[1,1,56]{2,1,0:T(1,128)S(1)}, s32[1,1,56]{2,1,0:T(1,128)}, u32[]{:S(2)}) copy-start(s32[1,1,56]{2,1,0:T(1,128)} %param.15) | copy-start | bytes 676
  7.2 80.4 %copy-start.4 = (s32[1,1,56]{2,1,0:T(1,128)S(1)}, s32[1,1,56]{2,1,0:T(1,128)}, u32[]{:S(2)}) copy-start(s32[1,1,56]{2,1,0:T(1,128)} %param.16) | copy-start | bytes 676
  7.2 80.4 %copy-start.2 = (bf16[1,1,56,128,128]{4,3,2,1,0:T(8,128)(2,1)S(1)}, bf16[1,1,56,128,128]{4,3,2,1,0:T(8,128)(2,1)}, u32[]{:S(2)}) copy-start(bf16[1,1,56,128,128]{4,3,2,1,0:T(8,128)(2,1)} %param.14) | copy-start | bytes 5505028
  7.2 78.8 %all-gather.4.cloned.1.call-start = ((), (), s32[]{:S(2)}) async-start(), calls=%async_computation.2 | async-start | bytes 2162688 | tf_op jit(solution)/shard_map/all_gather | solution.py:54
  7.9 211.9 %reduce-scatter.3.cloned.1.call-start = ((), (), s32[]{:S(2)}) async-start(), calls=%async_computation.3 | async-start | bytes 1114112 | tf_op jit(solution)/shard_map/reduce_scatter | solution.py:60
  114.2 2.8 copy-start.7
  114.2 105.6 %copy-start.5 = (bf16[1,128,256]{2,1,0:T(8,128)(2,1)S(1)}, bf16[1,128,256]{2,1,0:T(8,128)(2,1)}, u32[]{:S(2)}) copy-start(bf16[1,128,256]{2,1,0:T(8,128)(2,1)} %param.20) | copy-start | bytes 196612
  114.2 105.6 %copy-start.6 = (f32[256]{0:T(256)S(1)}, f32[256]{0:T(256)}, u32[]{:S(2)}) copy-start(f32[256]{0:T(256)} %param.19) | copy-start | bytes 3076
  117.0 316.6 %all-reduce.3.cloned.1.call-start = ((), (), s32[]{:S(2)}) async-start(), calls=%async_computation.4 | async-start | bytes 524288 | tf_op jit(solution)/shard_map/psum | solution.py:42
  223.3 271.1 %all-gather.6.cloned.1.call-start = ((), (), s32[]{:S(2)}) async-start(), calls=%async_computation.7 | async-start | bytes 1114112 | tf_op jit(solution)/shard_map/all_gather | solution.py:76
  224.2 394.8 %all-reduce.5.cloned.1.call-start = ((), (), s32[]{:S(2)}) async-start(), calls=%async_computation.5 | async-start | bytes 524288 | tf_op jit(solution)/shard_map/psum | solution.py:42
  433.6 294.0 %reduce-scatter.5.cloned.1.call-start = ((), (), s32[]{:S(2)}) async-start(), calls=%async_computation.6 | async-start | bytes 2162688 | tf_op jit(solution)/shard_map/reduce_scatter | solution.py:89
  494.4 2.4 copy-start.1
Sparse Core Ops, SparseCore 0:
  10.1 75.8 all-gather.3
  117.1 102.6 reduce-scatter.2
  223.4 210.0 all-reduce.2
  437.0 57.3 all-gather.5
  497.4 114.6 all-reduce.4
  615.3 112.2 reduce-scatter.4
